TPU v7x, 128 devices: a whole 4x4x4 slice. The times are simulated.
128 devices in a mesh: ep: 32 (over z, y, core), dp: 4 (over x).
Axes of the slice: x: 4, y: 4, z: 4, core: 2. Of those that a mesh axis runs over, the one named last changes fastest.
Arguments:
- tokens: bfloat16 [2048, 7168], P(('ep', 'dp')), may hold values from -6 to 6
- routes: int32 [2048, 8], P(('ep', 'dp')), may hold values from 0 to 31, all different within a row; in each aligned block of 16 rows (0 to 15, 16 to 31, ...) at most 8 rows name the same one
- route_logits: float32 [2048, 8], P(('ep', 'dp')), may hold values from -6 to 6
- gate_weight: bfloat16 [32, 7168, 2048], P('ep', None, 'dp'), may hold values from -0.0625 to 0.0625
- up_weight: bfloat16 [32, 7168, 2048], P('ep', None, 'dp'), may hold values from -0.0625 to 0.0625
- down_weight: bfloat16 [32, 2048, 7168], P('ep', 'dp'), may hold values from -0.125 to 0.125
Outputs:
- moe_output: bfloat16 [2048, 7168], P(('ep', 'dp'))
- expert_load: float32 [32], P('ep')
Inputs may be any that keep to these rules, and one draw needn't show every extreme that they name: `routes`: each row names 8 different experts. Within the rows of one device (aligned blocks of 16 rows) no expert is named more than 8 times, and in every draw some expert is named exactly 8 times there; every expert is named somewhere.
All inputs are finite; a program needn't handle non-finite values.
Results may differ from a plain program's by a relative error of at most 0.012.
Values may be sent and summed in bfloat16 or wider, within the bound.
No kernel may reach another device: no remote copies, remote signals or barrier semaphores. Data moves between devices by JAX's collectives and lax.ppermute only.
A program may use at most 128 MiB of HBM per device.

v0:
```python
import jax
import jax.numpy as jnp
from jax import lax
from jax.sharding import Mesh
from jax.sharding import PartitionSpec as P

EP = ("ep_0", "ep_1", "ep_2")
EP_DP = ("ep_0", "ep_1", "ep_2", "dp")
ROUTE_SCALE = 2.5
PRECISE = lax.Precision.HIGHEST


def split_up(x, dim, devices):
    before, after = (x.shape[:dim], x.shape[dim + 1 :])
    return jnp.moveaxis(x.reshape(*before, devices, -1, *after), dim, 0)


def laid_out(parts, dim):
    lengths = list(parts.shape[1:])
    lengths[dim] *= parts.shape[0]
    return jnp.moveaxis(parts, 0, dim).reshape(lengths)


def moved_by_axis(parts, axes, order):
    lengths = [lax.axis_size(a) for a in axes]
    parts = parts.reshape(*lengths, *parts.shape[1:])
    for k in order:
        parts = lax.all_to_all(parts, axes[k], split_axis=k, concat_axis=k, tiled=True)
    return parts.reshape(-1, *parts.shape[len(axes) :])


def core_and_chips(x, groups, order, split_dim, concat_dim):
    devices = lax.axis_size(groups[0]) * lax.axis_size(groups[1])
    parts = split_up(x, split_dim, devices)
    return laid_out(moved_by_axis(parts, groups, order), concat_dim)


def sum_at_owner(x, axis, dim):
    devices = lax.axis_size(axis)
    parts = lax.all_to_all(split_up(x, dim, devices), axis, 0, 0, tiled=True)
    return jnp.sum(parts, axis=0)


def sent_to_all(x, axis):
    copies = jnp.broadcast_to(x, (lax.axis_size(axis), *x.shape))
    return lax.all_to_all(copies, axis, split_axis=0, concat_axis=0, tiled=True)


def over_copies(x, axis):
    return sent_to_all(x, axis).sum(axis=0)


def assignment_slots(flat_routes, experts):
    labels = jnp.arange(experts, dtype=jnp.int32)
    onehot = (flat_routes[:, :, None] == labels[None, None, :]).astype(jnp.int32)
    before = jnp.cumsum(onehot, axis=1) - onehot
    return (jnp.sum(before * onehot, axis=2), jnp.sum(onehot, axis=1))


def pack(members, flat_routes, slot_ids, experts, capacity, top_k):
    blocks, per_block = flat_routes.shape
    tok_dev = per_block // top_k
    member = jnp.arange(blocks, dtype=jnp.int32)[:, None]
    target = ((member * experts + flat_routes) * capacity + slot_ids).reshape(-1)
    source = (member * tok_dev + jnp.arange(per_block, dtype=jnp.int32)[None, :] // top_k).reshape(
        -1
    )
    placing = (
        jnp.arange(blocks * experts * capacity, dtype=jnp.int32)[:, None] == target[None, :]
    ).astype(jnp.bfloat16)
    owners = (source[:, None] == jnp.arange(blocks * tok_dev, dtype=jnp.int32)[None, :]).astype(
        jnp.bfloat16
    )
    picker = jnp.dot(placing, owners, preferred_element_type=jnp.float32).astype(jnp.bfloat16)
    filled = jnp.dot(picker, members, preferred_element_type=jnp.float32).astype(jnp.bfloat16)
    return filled.reshape(blocks, experts, capacity, members.shape[1])


def expert_rows(row_block, gate_w, up_w, down_w):
    gate_act = jnp.dot(row_block, gate_w, preferred_element_type=jnp.float32)
    up_act = jnp.dot(row_block, up_w, preferred_element_type=jnp.float32)
    hidden = (jax.nn.silu(gate_act) * up_act).astype(jnp.bfloat16)
    return jnp.dot(hidden, down_w, preferred_element_type=jnp.float32)


def on_device(tokens, routes, route_logits, gate_weight, up_weight, down_weight):
    tok_dev, top_k = routes.shape
    model_width = tokens.shape[1]
    experts = lax.axis_size(EP)
    groups = lax.axis_size("dp")
    capacity = min(tok_dev // 2, 2 * tok_dev * top_k // experts)
    per_block = tok_dev * top_k
    gate_w = gate_weight[0]
    up_w = up_weight[0]
    down_w = down_weight[0]
    own_flat = routes.reshape(1, per_block)
    own_slots, own_counts = assignment_slots(own_flat, experts)
    buffer = pack(tokens, own_flat, own_slots, experts, capacity, top_k)
    received = core_and_chips(buffer, (("ep_0", "ep_1"), "ep_2"), (1, 0), 1, 1)
    partial_value = expert_rows(
        lax.all_gather(received.reshape(-1, model_width), "dp", axis=0, tiled=True),
        gate_w,
        up_w,
        down_w,
    )
    shares = lax.psum_scatter(
        partial_value.astype(jnp.bfloat16), "dp", scatter_dimension=0, tiled=True
    ).astype(jnp.float32)
    returned = lax.all_to_all(
        shares.reshape(experts, capacity, model_width).astype(jnp.bfloat16),
        EP,
        split_axis=0,
        concat_axis=0,
        tiled=True,
    ).astype(jnp.float32)
    affinity = jax.nn.sigmoid(route_logits)
    weights = (ROUTE_SCALE * affinity / jnp.sum(affinity, axis=1, keepdims=True)).reshape(-1)
    own_target = own_flat[0] * capacity + own_slots[0]
    spread = jnp.where(
        own_target[:, None] == jnp.arange(experts * capacity, dtype=jnp.int32)[None, :],
        weights[:, None],
        0.0,
    )
    owners = (
        jnp.arange(tok_dev, dtype=jnp.int32)[:, None]
        == jnp.arange(per_block, dtype=jnp.int32)[None, :] // top_k
    ).astype(jnp.float32)
    combine = jnp.dot(owners, spread, precision=PRECISE)
    moe_output = jnp.dot(
        combine, returned.reshape(experts * capacity, model_width), precision=PRECISE
    ).astype(jnp.bfloat16)
    local_counts = own_counts[0].astype(jnp.float32)
    group_count = sum_at_owner(local_counts, EP, 0)
    expert_count = over_copies(group_count, "dp")
    mean_count = float(tok_dev * groups * top_k)
    expert_load = expert_count / mean_count
    return (moe_output, expert_load)


def solution(mesh):
    finer = Mesh(mesh.devices.reshape(4, 4, 2, mesh.shape["dp"]), ("ep_0", "ep_1", "ep_2", "dp"))
    in_specs = (
        P(EP_DP, None),
        P(EP_DP, None),
        P(EP_DP, None),
        P(EP, None, "dp"),
        P(EP, None, "dp"),
        P(EP, "dp", None),
    )
    out_specs = (P(EP_DP, None), P(EP))
    return jax.shard_map(
        on_device, mesh=finer, in_specs=in_specs, out_specs=out_specs, check_vma=False
    )
```

profile of v0, /device:TPU:0, one launch (start us, length us, event | category | flops | bytes accessed | tf_op | source)
XLA Modules:
  0.0 443.3 jit_solution(7559866327238742268)
XLA Ops:
  7.2 0.0 copy-start
  7.2 0.0 all-gather.2.cloned.1.call-start
  7.2 0.8 copy.22
  8.0 0.1 squeeze_reshape.3
  8.1 0.1 fusion.15
  8.2 0.2 reduce_window_sum.11
  8.4 0.2 fusion.16
  8.6 0.0 copy-done
  8.6 3.2 convolution_convert_fusion.1
  11.8 2.3 copy.24
  14.1 6.7 %all_to_all.27 = bf16[16,2,1,1,8,7168]{5,4,0,3,2,1:T(8,128)(2,1)S(1)} all-to-all(bf16[16,2,1,1,8,7168]{5,4,0,3,2,1:T(8,128)(2,1)S(1)} %copy.24), channel_id=1, replica_groups=mesh['ep_0'=4,'ep_1'=4,'ep_2'=2,'dp'=4] {'ep_2'}, dimensions={1} | all-to-all | bytes 7340032 | tf_op jit(solution)/shard_map/all_to_all | solution.py:28
  20.8 0.3 copy.25
  21.1 53.6 %all_to_all.28 = bf16[16,2,1,1,8,7168]{5,4,1,3,2,0:T(8,128)(2,1)} all-to-all(bf16[16,2,1,1,8,7168]{5,4,1,3,2,0:T(8,128)(2,1)S(1)} %copy.25), channel_id=1, replica_groups=mesh['ep_0'=4,'ep_1'=4,'ep_2'=2,'dp'=4] {'ep_0','ep_1'}, dimensions={0} | all-to-all | bytes 7340032 | tf_op jit(solution)/shard_map/all_to_all | solution.py:28
  74.7 0.0 all-gather.2.cloned.1.call-update
  74.7 0.0 reduce-scatter.2.cloned.1.call-start
  74.7 133.9 %all-gather.2.cloned.1.call-done = bf16[1024,7168]{1,0:T(8,128)(2,1)} async-done(((bf16[256,7168]{1,0:T(8,128)(2,1)}), bf16[1024,7168]{1,0:T(8,128)(2,1)}) %all-gather.2.cloned.1.call-update) | async-done | bytes 14680080 | tf_op jit(solution)/shard_map/all_gather | solution.py:101
  208.6 0.0 copy-start.3
  208.6 0.0 slice-start
  208.7 13.4 %fusion.1 = f32[1024,512]{1,0:T(8,128)S(1)} fusion(bf16[1024,7168]{1,0:T(8,128)(2,1)} %all-gather.2.cloned.1.call-done, bf16[1,7168,512]{2,1,0:T(8,128)(2,1)} %param.10), kind=kOutput, calls=%fused_computation.4 | convolution fusion | flops 7516192768 | bytes 24117248 | tf_op jit(solution)/shard_map/dot_general | solution.py:81
  222.0 0.0 copy-done.3
  222.0 0.0 slice-start.1
  222.0 10.3 %multiply_convert_fusion = bf16[1024,512]{1,0:T(8,128)(2,1)S(1)} fusion(f32[1024,512]{1,0:T(8,128)S(1)} %fusion.1, bf16[1024,7168]{1,0:T(8,128)(2,1)S(1)} %copy-done.3, bf16[1,7168,512]{2,1,0:T(8,128)(2,1)} %param.9), kind=kOutput, calls=%fused_computation.9 | convolution fusion | flops 7519338496 | bytes 25165824 | tf_op jit(solution)/shard_map/dot_general | solution.py:80
  232.3 0.0 slice-done
  232.3 0.0 slice-done.1
  232.3 11.1 %convolution_convert_fusion = bf16[1024,7168]{1,0:T(8,128)(2,1)} fusion(bf16[1024,512]{1,0:T(8,128)(2,1)S(1)} %multiply_convert_fusion, bf16[1,512,7168]{2,1,0:T(8,128)(2,1)S(1)} %bitcast.29), kind=kOutput, calls=%fused_computation | convolution fusion | flops 7523532800 | bytes 23068672 | tf_op jit(solution)/shard_map/dot_general | solution.py:83
  243.4 0.0 reduce-scatter.2.cloned.1.call-update
  243.4 0.0 copy-start.2
  243.4 0.0 copy-start.1
  243.5 0.1 copy.26
  243.5 14.5 %all_to_all.29 = f32[32,1,1]{2,1,0:T(1,128)S(1)} all-to-all(f32[32,1,1]{2,1,0:T(1,128)S(1)} %copy.26), channel_id=1, replica_groups=mesh['ep_0'=4,'ep_1'=4,'ep_2'=2,'dp'=4] {'ep_0','ep_1','ep_2'}, dimensions={0} | all-to-all | bytes 256 | tf_op jit(solution)/shard_map/all_to_all | solution.py:40
  258.1 0.6 reduce_sum.48
  258.7 0.6 broadcast_in_dim.29
  259.4 9.0 %all_to_all.30 = f32[4,1,1]{2,1,0:T(1,128)S(1)} all-to-all(f32[4,1,1]{2,1,0:T(1,128)S(1)} %broadcast_in_dim.29), channel_id=1, replica_groups=mesh['ep_0'=4,'ep_1'=4,'ep_2'=2,'dp'=4] {'dp'}, dimensions={0} | all-to-all | bytes 32 | tf_op jit(solution)/shard_map/all_to_all | solution.py:46
  268.4 107.6 %reduce-scatter.2.cloned.1.call-done = bf16[256,7168]{1,0:T(8,128)(2,1)} async-done(((bf16[1024,7168]{1,0:T(8,128)(2,1)}), bf16[256,7168]{1,0:T(8,128)(2,1)}) %reduce-scatter.2.cloned.1.call-update) | async-done | bytes 3670032 | tf_op jit(solution)/shard_map/reduce_scatter | solution.py:106
  376.0 7.4 %all-to-all-start.2 = ((bf16[32,8,7168]{2,1,0:T(8,128)(2,1)}), bf16[32,8,7168]{2,1,0:T(8,128)(2,1)}, u32[]{:S(2)}, u32[]{:S(2)}) async-start(bf16[32,8,7168]{2,1,0:T(8,128)(2,1)} %bitcast.27), calls=%async_computation.3 | async-start | bytes 7340032 | tf_op jit(solution)/shard_map/all_to_all | solution.py:109
  383.4 0.0 copy-done.2
  383.4 0.1 copy.23
  383.5 0.1 broadcast_in_dim.16
  383.6 0.2 fusion.8
  383.8 0.6 reduce_sum.49
  385.1 45.9 %all-to-all-done.2 = bf16[32,8,7168]{2,1,0:T(8,128)(2,1)} async-done(((bf16[32,8,7168]{2,1,0:T(8,128)(2,1)}), bf16[32,8,7168]{2,1,0:T(8,128)(2,1)}, u32[]{:S(2)}, u32[]{:S(2)}) %all-to-all-start.2) | async-done | bytes 3670048 | tf_op jit(solution)/shard_map/all_to_all | solution.py:109
  431.1 4.3 convolution_convert_fusion.2
  435.3 0.0 copy-done.1
  (6 shorter events, 0.1 us)
Async XLA Ops:
  7.2 1.4 copy-start
  7.2 201.5 %all-gather.2.cloned.1.call-start = ((), (), s32[]{:S(2)}) async-start(), calls=%async_computation.6 | async-start | bytes 18350080 | tf_op jit(solution)/shard_map/all_gather | solution.py:101
  74.7 301.3 %reduce-scatter.2.cloned.1.call-start = ((), (), s32[]{:S(2)}) async-start(), calls=%async_computation.7 | async-start | bytes 18350080 | tf_op jit(solution)/shard_map/reduce_scatter | solution.py:106
  208.6 13.4 %copy-start.3 = (bf16[1024,7168]{1,0:T(8,128)(2,1)S(1)}, bf16[1024,7168]{1,0:T(8,128)(2,1)}, u32[]{:S(2)}) copy-start(bf16[1024,7168]{1,0:T(8,128)(2,1)} %all-gather.2.cloned.1.call-done) | copy-start | bytes 44040196
  208.6 23.7 %slice-start = ((s8[7340032]{0:T(1024)(128)(4,1)}), s8[4194304]{0:T(1024)(128)(4,1)S(1)}, s32[]{:S(2)}) async-start(s8[7340032]{0:T(1024)(128)(4,1)} %bitcast.28), calls=%async_computation.8 | async-start | bytes 8388608
  222.0 10.3 %slice-start.1 = ((s8[7340032]{0:T(1024)(128)(4,1)}), s8[3145728]{0:T(1024)(128)(4,1)S(1)}, s32[]{:S(2)}) async-start(s8[7340032]{0:T(1024)(128)(4,1)} %bitcast.28), calls=%async_computation.9 | async-start | bytes 6291456
  243.4 140.0 %copy-start.2 = (f32[16,8]{0,1:T(8,128)S(1)}, f32[16,8]{0,1:T(8,128)}, u32[]{:S(2)}) copy-start(f32[16,8]{0,1:T(8,128)} %param.8) | copy-start | bytes 1540
  243.4 191.9 %copy-start.1 = (bf16[16,7168]{1,0:T(8,128)(2,1)S(1)}, bf16[16,7168]{1,0:T(8,128)(2,1)}, u32[]{:S(2)}) copy-start(bf16[16,7168]{1,0:T(8,128)(2,1)} %param.6) | copy-start | bytes 688132
  376.0 55.1 %all-to-all-start.2 = ((bf16[32,8,7168]{2,1,0:T(8,128)(2,1)}), bf16[32,8,7168]{2,1,0:T(8,128)(2,1)}, u32[]{:S(2)}, u32[]{:S(2)}) async-start(bf16[32,8,7168]{2,1,0:T(8,128)(2,1)} %bitcast.27), calls=%async_computation.3 | async-start | bytes 7340032 | tf_op jit(solution)/shard_map/all_to_all | solution.py:109
Sparse Core Ops, SparseCore 0:
  74.8 133.7 all-gather.1
  243.5 132.4 reduce-scatter.1
where the time goes:
time: 444 us; the launch traced here: 443 us
  waiting for transfers between devices  288 us (65%)
  blocking collectives  83.8 us (19%)
  matrix products  42.4 us (10%)
  between operations  16 us (4%)
  starting transfers between devices  7.45 us (2%)
    all_gather x1, waiting for transfers between devices, on_device(): lax.all_gather(received.reshape(-1, model_width), 'dp', axis=0, tiled=True)  134 us
    reduce_scatter x1, waiting for transfers between devices, on_device(): lax.psum_scatter(partial_value.astype(jnp.bfloat16), 'dp', scatter_dimens...  108 us
    all_to_all x2, blocking collectives, moved_by_axis(): lax.all_to_all(parts, axes[k], split_axis=k, concat_axis=k, tiled=True)  60.3 us
    all_to_all x1, waiting for transfers between devices, on_device(): lax.all_to_all(shares.reshape(experts, capacity, model_width).astype(jnp....  45.9 us
    all_to_all x1, blocking collectives, sum_at_owner(): parts = lax.all_to_all(split_up(x, dim, devices), axis, 0, 0, tiled=True)  14.5 us
    dot_general x1, matrix products, expert_rows(): up_act = jnp.dot(row_block, up_w, preferred_element_type=jnp.float32)  13.4 us
    dot_general x1, matrix products, expert_rows(): return jnp.dot(hidden, down_w, preferred_element_type=jnp.float32)  11.1 us
    dot_general x1, matrix products, expert_rows(): gate_act = jnp.dot(row_block, gate_w, preferred_element_type=jnp.float32)  10.3 us
  transfers between devices with their start and end apart: 3, of which 3 were waited for; matrix products, arithmetic and copies ran while one was open for 1% of the time, Pallas kernels for 0%

commit v1 on v0

--- a/solution.py
+++ b/solution.py
@@ -1,13 +1,26 @@
+import functools
 import jax
 import jax.numpy as jnp
 from jax import lax
 from jax.sharding import Mesh
 from jax.sharding import PartitionSpec as P
+from jax.lax import all_to_all, axis_size
 
 EP = ("ep_0", "ep_1", "ep_2")
 EP_DP = ("ep_0", "ep_1", "ep_2", "dp")
 ROUTE_SCALE = 2.5
 PRECISE = lax.Precision.HIGHEST
+
+
+def direct_keys(v0, dim_k):
+    known = axis_size("dp")
+    d_next = jnp.stack([v0] * known, 0)
+    kept_arr = all_to_all(d_next, "dp", 0, 0)
+    clean = jnp.concatenate(kept_arr, dim_k)
+    return clean
+
+
+lay_the_domain = functools.partial(direct_keys, dim_k=0)
 
 
 def split_up(x, dim, devices):
@@ -98,10 +111,7 @@
     buffer = pack(tokens, own_flat, own_slots, experts, capacity, top_k)
     received = core_and_chips(buffer, (("ep_0", "ep_1"), "ep_2"), (1, 0), 1, 1)
     partial_value = expert_rows(
-        lax.all_gather(received.reshape(-1, model_width), "dp", axis=0, tiled=True),
-        gate_w,
-        up_w,
-        down_w,
+        lay_the_domain(received.reshape(-1, model_width)), gate_w, up_w, down_w
     )
     shares = lax.psum_scatter(
         partial_value.astype(jnp.bfloat16), "dp", scatter_dimension=0, tiled=True

time: 444 us -> 469 us (1.056)
  blocking collectives: 83.8 us -> 243 us
  waiting for transfers between devices: 288 us -> 153 us
    all_to_all x0 -> x1, blocking collectives: none -> 164 us  [direct_keys(): kept_arr = all_to_all(d_next, 'dp', 0, 0)]
    all_gather x1 -> x0, waiting for transfers between devices: 134 us -> none  [on_device(): lax.all_gather(received.reshape(-1, model_width), 'dp', axis=0, tiled=True)]
    dot_general x1, matrix products: 13.4 us -> 7.71 us  [expert_rows(): up_act = jnp.dot(row_block, up_w, preferred_element_type=jnp.float32)]
  transfers between devices with their start and end apart: 3 -> 2, of which waited for: 3 -> 2; matrix products, arithmetic and copies ran while one was open for 1% -> 1% of each run, Pallas kernels for 0% -> 0%
where the time goes in v1:
time: 469 us; the launch traced here: 468 us
  blocking collectives  243 us (52%)
  waiting for transfers between devices  153 us (33%)
  matrix products  39.7 us (8%)
  between operations  16 us (3%)
  starting transfers between devices  7.43 us (2%)
  local copies, waits for them, and re-layouts  6.33 us (1%)
    all_to_all x1, blocking collectives, direct_keys(): kept_arr = all_to_all(d_next, 'dp', 0, 0)  164 us
    reduce_scatter x1, waiting for transfers between devices, on_device(): lax.psum_scatter(partial_value.astype(jnp.bfloat16), 'dp', scatter_dimens...  108 us
    all_to_all x2, blocking collectives, moved_by_axis(): lax.all_to_all(parts, axes[k], split_axis=k, concat_axis=k, tiled=True)  60.2 us
    all_to_all x1, waiting for transfers between devices, on_device(): lax.all_to_all(shares.reshape(experts, capacity, model_width).astype(jnp....  45.9 us
    dot_general x1, matrix products, expert_rows(): return jnp.dot(hidden, down_w, preferred_element_type=jnp.float32)  14.1 us
    all_to_all x1, blocking collectives, sum_at_owner(): parts = lax.all_to_all(split_up(x, dim, devices), axis, 0, 0, tiled=True)  11.3 us
    dot_general x1, matrix products, expert_rows(): gate_act = jnp.dot(row_block, gate_w, preferred_element_type=jnp.float32)  10.2 us
  transfers between devices with their start and end apart: 2, of which 2 were waited for; matrix products, arithmetic and copies ran while one was open for 1% of the time, Pallas kernels for 0%

profile of v1, /device:TPU:0, one launch (start us, length us, event | category | flops | bytes accessed | tf_op | source)
XLA Modules:
  0.0 468.1 jit_solution(11718152369794525964)
XLA Ops:
  7.2 0.0 copy-start
  7.2 0.0 reduce-scatter.2.cloned.1.call-start
  7.2 0.8 copy.22
  8.0 0.1 squeeze_reshape.3
  8.1 0.1 fusion.15
  8.2 0.2 reduce_window_sum.11
  8.4 0.2 fusion.16
  8.6 0.0 copy-done
  8.6 3.2 convolution_convert_fusion.1
  11.8 2.3 copy.24
  14.1 6.7 %all_to_all.32 = bf16[16,2,1,1,8,7168]{5,4,0,3,2,1:T(8,128)(2,1)S(1)} all-to-all(bf16[16,2,1,1,8,7168]{5,4,0,3,2,1:T(8,128)(2,1)S(1)} %copy.24), channel_id=1, replica_groups=mesh['ep_0'=4,'ep_1'=4,'ep_2'=2,'dp'=4] {'ep_2'}, dimensions={1} | all-to-all | bytes 7340032 | tf_op jit(solution)/shard_map/all_to_all | solution.py:41
  20.8 0.3 copy.25
  21.1 53.5 %all_to_all.33 = bf16[16,2,1,1,8,7168]{5,4,1,3,2,0:T(8,128)(2,1)S(1)} all-to-all(bf16[16,2,1,1,8,7168]{5,4,1,3,2,0:T(8,128)(2,1)S(1)} %copy.25), channel_id=1, replica_groups=mesh['ep_0'=4,'ep_1'=4,'ep_2'=2,'dp'=4] {'ep_0','ep_1'}, dimensions={0} | all-to-all | bytes 7340032 | tf_op jit(solution)/shard_map/all_to_all | solution.py:41
  74.6 0.0 slice-start
  74.6 1.9 stack.3
  76.5 0.0 slice-start.1
  76.5 164.4 %all_to_all.34 = bf16[4,256,7168]{2,1,0:T(8,128)(2,1)S(1)} all-to-all(bf16[4,256,7168]{2,1,0:T(8,128)(2,1)S(1)} %stack.3), channel_id=1, replica_groups=mesh['ep_0'=4,'ep_1'=4,'ep_2'=2,'dp'=4] {'dp'}, dimensions={0} | all-to-all | bytes 29360128 | tf_op jit(solution)/shard_map/all_to_all | solution.py:18
  240.9 0.0 slice-done
  240.9 0.0 slice-done.1
  240.9 7.7 %fusion.1 = f32[1024,512]{1,0:T(8,128)S(1)} fusion(bf16[1024,7168]{1,0:T(8,128)(2,1)S(1)} %bitcast.26, bf16[1,7168,512]{2,1,0:T(8,128)(2,1)S(1)} %bitcast.32), kind=kOutput, calls=%fused_computation.4 | convolution fusion | flops 7516192768 | bytes 24117248 | tf_op jit(solution)/shard_map/dot_general | solution.py:94
  248.6 10.2 %multiply_convert_fusion = bf16[1024,512]{1,0:T(8,128)(2,1)S(1)} fusion(f32[1024,512]{1,0:T(8,128)S(1)} %fusion.1, bf16[1024,7168]{1,0:T(8,128)(2,1)S(1)} %bitcast.27, bf16[1,7168,512]{2,1,0:T(8,128)(2,1)} %param.9), kind=kOutput, calls=%fused_computation.9 | convolution fusion | flops 7519338496 | bytes 25165824 | tf_op jit(solution)/shard_map/dot_general | solution.py:93
  258.8 14.1 %convolution_convert_fusion = bf16[1024,7168]{1,0:T(8,128)(2,1)} fusion(bf16[1024,512]{1,0:T(8,128)(2,1)S(1)} %multiply_convert_fusion, bf16[1,512,7168]{2,1,0:T(8,128)(2,1)} %param.11), kind=kOutput, calls=%fused_computation | convolution fusion | flops 7523532800 | bytes 23068672 | tf_op jit(solution)/shard_map/dot_general | solution.py:96
  272.9 0.0 reduce-scatter.2.cloned.1.call-update
  272.9 0.0 copy-start.2
  272.9 0.0 copy-start.1
  273.0 0.1 copy.26
  273.0 11.3 %all_to_all.35 = f32[32,1,1]{2,1,0:T(1,128)S(1)} all-to-all(f32[32,1,1]{2,1,0:T(1,128)S(1)} %copy.26), channel_id=1, replica_groups=mesh['ep_0'=4,'ep_1'=4,'ep_2'=2,'dp'=4] {'ep_0','ep_1','ep_2'}, dimensions={0} | all-to-all | bytes 256 | tf_op jit(solution)/shard_map/all_to_all | solution.py:53
  284.3 0.6 reduce_sum.48
  285.0 0.6 broadcast_in_dim.29
  285.6 7.6 %all_to_all.36 = f32[4,1,1]{2,1,0:T(1,128)S(1)} all-to-all(f32[4,1,1]{2,1,0:T(1,128)S(1)} %broadcast_in_dim.29), channel_id=1, replica_groups=mesh['ep_0'=4,'ep_1'=4,'ep_2'=2,'dp'=4] {'dp'}, dimensions={0} | all-to-all | bytes 32 | tf_op jit(solution)/shard_map/all_to_all | solution.py:59
  293.2 107.5 %reduce-scatter.2.cloned.1.call-done = bf16[256,7168]{1,0:T(8,128)(2,1)} async-done(((bf16[1024,7168]{1,0:T(8,128)(2,1)}), bf16[256,7168]{1,0:T(8,128)(2,1)}) %reduce-scatter.2.cloned.1.call-update) | async-done | bytes 3670032 | tf_op jit(solution)/shard_map/reduce_scatter | solution.py:116
  400.8 7.4 %all-to-all-start.3 = ((bf16[32,8,7168]{2,1,0:T(8,128)(2,1)}), bf16[32,8,7168]{2,1,0:T(8,128)(2,1)}, u32[]{:S(2)}, u32[]{:S(2)}) async-start(bf16[32,8,7168]{2,1,0:T(8,128)(2,1)} %bitcast.30), calls=%async_computation.4 | async-start | bytes 7340032 | tf_op jit(solution)/shard_map/all_to_all | solution.py:119
  408.2 0.0 copy-done.2
  408.2 0.1 copy.23
  408.3 0.1 broadcast_in_dim.16
  408.4 0.2 fusion.8
  408.6 0.6 reduce_sum.49
  409.9 45.9 %all-to-all-done.3 = bf16[32,8,7168]{2,1,0:T(8,128)(2,1)} async-done(((bf16[32,8,7168]{2,1,0:T(8,128)(2,1)}), bf16[32,8,7168]{2,1,0:T(8,128)(2,1)}, u32[]{:S(2)}, u32[]{:S(2)}) %all-to-all-start.3) | async-done | bytes 3670048 | tf_op jit(solution)/shard_map/all_to_all | solution.py:119
  455.8 4.3 convolution_convert_fusion.2
  460.1 0.0 copy-done.1
  (6 shorter events, 0.1 us)
Async XLA Ops:
  7.2 1.4 copy-start
  7.2 393.6 %reduce-scatter.2.cloned.1.call-start = ((), (), s32[]{:S(2)}) async-start(), calls=%async_computation.7 | async-start | bytes 18350080 | tf_op jit(solution)/shard_map/reduce_scatter | solution.py:116
  74.6 166.4 %slice-start = ((s8[7340032]{0:T(1024)(128)(4,1)}), s8[4194304]{0:T(1024)(128)(4,1)S(1)}, s32[]{:S(2)}) async-start(s8[7340032]{0:T(1024)(128)(4,1)} %bitcast.31), calls=%async_computation.8 | async-start | bytes 8388608
  76.5 164.4 %slice-start.1 = ((s8[7340032]{0:T(1024)(128)(4,1)}), s8[3145728]{0:T(1024)(128)(4,1)S(1)}, s32[]{:S(2)}) async-start(s8[7340032]{0:T(1024)(128)(4,1)} %bitcast.31), calls=%async_computation.9 | async-start | bytes 6291456
  272.9 135.2 %copy-start.2 = (f32[16,8]{0,1:T(8,128)S(1)}, f32[16,8]{0,1:T(8,128)}, u32[]{:S(2)}) copy-start(f32[16,8]{0,1:T(8,128)} %param.8) | copy-start | bytes 1540
  272.9 187.2 %copy-start.1 = (bf16[16,7168]{1,0:T(8,128)(2,1)S(1)}, bf16[16,7168]{1,0:T(8,128)(2,1)}, u32[]{:S(2)}) copy-start(bf16[16,7168]{1,0:T(8,128)(2,1)} %param.6) | copy-start | bytes 688132
  400.8 55.1 %all-to-all-start.3 = ((bf16[32,8,7168]{2,1,0:T(8,128)(2,1)}), bf16[32,8,7168]{2,1,0:T(8,128)(2,1)}, u32[]{:S(2)}, u32[]{:S(2)}) async-start(bf16[32,8,7168]{2,1,0:T(8,128)(2,1)} %bitcast.30), calls=%async_computation.4 | async-start | bytes 7340032 | tf_op jit(solution)/shard_map/all_to_all | solution.py:119
Sparse Core Ops, SparseCore 0:
  273.0 127.6 reduce-scatter.1
